TPU v7x, 256 devices: a whole 4x4x8 slice. The times are simulated.
256 devices in a mesh: wide: 32 (over z, y), slab: 8 (over x, core).
Axes of the slice: x: 4, y: 4, z: 8, core: 2. Of those that a mesh axis runs over, the one named last changes fastest.
Arguments:
- thermal_state: float32 [32, 128, 32, 1024], P('wide', 'slab'), may hold values from -5 to 5
- thermal_spreading_rate: bfloat16 [32, 128, 32, 1024], P('wide', 'slab'), may hold values from 0.5 to 1.5
- flow_speed_vector: bfloat16 [3, 32, 128, 32, 1024], P(None, 'wide', 'slab'), may hold values from -0.796875 to 0.796875
- interface_guess: float32 [32, 2048], P('wide', 'slab'), may hold values from -4 to 4
- partner_facing_rows: int32 [32, 2048], P('wide', 'slab'), may hold values from 0 to 2047, each once within a row
- mismatch_change_matrix: float32 [32, 2048, 128], P('wide', 'slab'), may hold values from -5 to 5
- output_change_matrix: float32 [32, 2048, 128], P('wide', 'slab'), may hold values from -1.8 to 1.8
Outputs:
- temperature_out: float32 [32, 128, 32, 1024], P('wide', 'slab')
- updated_interface_guess: float32 [32, 2048], P('wide', 'slab')
- unitary_basis_factor: float32 [32, 2048, 128], P('wide', 'slab')
Inputs may be any that keep to these rules, and one draw needn't show every extreme that they name: `partner_facing_rows`: each partition's rows of matching are a permutation of its partner's interface rows.
All inputs are finite; a program needn't handle non-finite values.
Results may differ from a plain program's by a relative error of at most 0.0003.
Values may be sent and summed in bfloat16 or wider, within the bound.
No kernel may reach another device: no remote copies, remote signals or barrier semaphores. Data moves between devices by JAX's collectives and lax.ppermute only.
A program may use at most 64 MiB of HBM per device.

v0:
```python
import math
import jax
import jax.numpy as jnp
from jax import lax
from jax.sharding import PartitionSpec as P

INTERFACE_STRIP = 64
SWEEPS = 4
STEP_SIZE = 0.11


def padded(cells, sides, width):
    for axis, dim in sides:
        count = lax.axis_size(axis)
        ends = count - 1
        head = lax.slice_in_dim(cells, 0, width, axis=dim)
        tail = lax.slice_in_dim(cells, cells.shape[dim] - width, cells.shape[dim], axis=dim)
        cells = jnp.concatenate(
            [
                lax.ppermute(tail, axis, [(i, (i + 1) % count) for i in range(ends)]),
                cells,
                lax.ppermute(head, axis, [((i + 1) % count, i) for i in range(ends)]),
            ],
            axis=dim,
        )
    return cells


def partner(value, axis, stride):
    mask = 2**stride
    pairs = [(source, source ^ mask) for source in range(lax.axis_size(axis))]
    return lax.ppermute(value, axis, pairs)


def gather_sum(value, axes):
    count = lax.axis_size(axes)
    copies = jnp.broadcast_to(value[None], (count, *value.shape))
    return jnp.sum(lax.all_to_all(copies, axes, 0, 0, tiled=True), axis=0)


def sum_everywhere(square):
    rows = square.shape[0] // lax.axis_size("slab")
    blocks = square.reshape(-1, rows, square.shape[1])
    mine = jnp.sum(lax.all_to_all(blocks, "slab", 0, 0, tiled=True), axis=0)
    mine = gather_sum(mine, "wide")
    copies = jnp.broadcast_to(mine[None], blocks.shape)
    return lax.all_to_all(copies, "slab", 0, 0, tiled=True).reshape(square.shape)


def surround_wrapper(block_rows, mirror_layer):
    bottom = jnp.zeros((block_rows.shape[0], 1, block_rows.shape[2]), block_rows.dtype)
    stacked = jnp.concatenate([bottom, block_rows, mirror_layer[:, None, :]], axis=1)
    return jnp.pad(stacked, ((0, 0), (0, 0), (1, 1)))


def march_forward(bordered_array, diffuse_subdomain, subdomain_flow_speed):
    centre = bordered_array[1:-1, 1:-1, 1:-1]
    plus_first = bordered_array[2:, 1:-1, 1:-1]
    minus_first = bordered_array[:-2, 1:-1, 1:-1]
    plus_second = bordered_array[1:-1, 2:, 1:-1]
    minus_second = bordered_array[1:-1, :-2, 1:-1]
    plus_third = bordered_array[1:-1, 1:-1, 2:]
    minus_third = bordered_array[1:-1, 1:-1, :-2]
    spread = (
        plus_first
        + minus_first
        + plus_second
        + minus_second
        + plus_third
        + minus_third
        - 6.0 * centre
    )
    carried = 0.5 * (
        subdomain_flow_speed[0].astype(jnp.float32) * (plus_first - minus_first)
        + subdomain_flow_speed[1].astype(jnp.float32) * (plus_second - minus_second)
        + subdomain_flow_speed[2].astype(jnp.float32) * (plus_third - minus_third)
    )
    return centre + STEP_SIZE * (diffuse_subdomain.astype(jnp.float32) * spread - carried)


def shards(
    thermal_state,
    thermal_spreading_rate,
    flow_speed_vector,
    interface_guess,
    partner_facing_rows,
    mismatch_change_matrix,
    output_change_matrix,
):
    subdomain_thermal_state = thermal_state[0]
    diffuse_subdomain = thermal_spreading_rate[0]
    subdomain_flow_speed = flow_speed_vector[:, 0]
    layer_stack = subdomain_thermal_state.shape[0]
    vertical_extent = subdomain_thermal_state.shape[1]
    rows_dev = interface_guess.shape[1]
    mirror_layer = jnp.repeat(interface_guess[0].reshape(layer_stack, -1), INTERFACE_STRIP, axis=1)
    panel = mismatch_change_matrix[0]
    gram_local = lax.dot_general(
        panel,
        panel,
        (((0,), (0,)), ((), ())),
        precision=lax.Precision.HIGHEST,
        preferred_element_type=jnp.float32,
    )
    ghost_padded = jnp.pad(mirror_layer, ((1, 1), (0, 0)))
    for sweep in range(SWEEPS):
        widened_array = padded(subdomain_thermal_state, (("slab", 0),), 1)
        subdomain_thermal_state = march_forward(
            surround_wrapper(widened_array, ghost_padded), diffuse_subdomain, subdomain_flow_speed
        )
    face_means = jnp.mean(
        subdomain_thermal_state[:, vertical_extent - 1, :].reshape(
            layer_stack, -1, INTERFACE_STRIP
        ),
        axis=2,
    )
    face_means = face_means.reshape(1, rows_dev)
    top_bit = lax.axis_size("wide").bit_length() - 2
    partner_own = partner(face_means, "wide", top_bit)
    partner_all = lax.all_gather(partner_own, "slab", axis=1, tiled=True)
    tilde = jnp.take(partner_all[0], partner_facing_rows[0], axis=0)
    resid = tilde - interface_guess[0]
    proj_local = jnp.dot(
        resid, panel, precision=lax.Precision.HIGHEST, preferred_element_type=jnp.float32
    )
    gram_matrix = sum_everywhere(gram_local)
    projection = gather_sum(proj_local, ("wide", "slab"))
    lower_factor = jnp.linalg.cholesky(gram_matrix)
    half_solve = lax.linalg.triangular_solve(
        lower_factor, projection[:, None], left_side=True, lower=True
    )
    coefficients = -lax.linalg.triangular_solve(
        lower_factor, half_solve, left_side=True, lower=True, transpose_a=True
    )[:, 0]
    update = jnp.dot(
        output_change_matrix[0],
        coefficients,
        precision=lax.Precision.HIGHEST,
        preferred_element_type=jnp.float32,
    )
    updated_interface_guess = tilde + update
    total_rows = rows_dev * lax.axis_size("slab") * lax.axis_size("wide")
    scaled = lax.linalg.triangular_solve(
        lower_factor, panel, left_side=False, lower=True, transpose_a=True
    )
    unitary_basis_factor = math.sqrt(total_rows) * scaled
    return (
        subdomain_thermal_state[None],
        updated_interface_guess[None],
        unitary_basis_factor[None],
    )


def solution(mesh):
    return jax.shard_map(
        shards,
        mesh=mesh,
        in_specs=(
            P("wide", "slab", None, None),
            P("wide", "slab", None, None),
            P(None, "wide", "slab", None, None),
            P("wide", "slab"),
            P("wide", "slab"),
            P("wide", "slab", None),
            P("wide", "slab", None),
        ),
        out_specs=(P("wide", "slab", None, None), P("wide", "slab"), P("wide", "slab", None)),
        check_vma=False,
    )
```

profile of v0, /device:TPU:1, one launch (start us, length us, event | category | flops | bytes accessed | tf_op | source)
XLA Modules:
  0.0 155.6 jit_solution(3249432732262084621)
XLA Ops:
  0.6 1.0 slice_bitcast_fusion
  1.7 5.1 %collective-permute-start = (f32[1,32,1024]{2,1,0:T(8,128)S(1)}, f32[1,32,1024]{2,1,0:T(8,128)S(1)}, u32[]{:S(2)}, u32[]{:S(2)}) collective-permute-start(f32[1,32,1024]{2,1,0:T(8,128)S(1)} %get-tuple-element.22), channel_id=1, source_target_pairs={{1,0},{2,1},{3,2},{4,3},{5,4},{6,5},{7,6},{9,8},{10,9},{11,10},{12... | collective-permute-start | bytes 393224 | tf_op jit(solution)/shard_map/ppermute | solution.py:22
  6.8 1.9 %collective-permute-start.1 = (f32[1,32,1024]{2,1,0:T(8,128)S(1)}, f32[1,32,1024]{2,1,0:T(8,128)S(1)}, u32[]{:S(2)}, u32[]{:S(2)}) collective-permute-start(f32[1,32,1024]{2,1,0:T(8,128)S(1)} %get-tuple-element.21), channel_id=1, source_target_pairs={{0,1},{1,2},{2,3},{3,4},{4,5},{5,6},{6,7},{8,9},{9,10},{10,11},{11... | collective-permute-start | bytes 393224 | tf_op jit(solution)/shard_map/ppermute | solution.py:20
  9.3 1.3 reduce.12
  11.0 0.7 copy-done.15
  11.7 2.3 %pad_maximum_fusion.3 = f32[18,34,1024]{2,1,0:T(8,128)S(1)} fusion(f32[18,1,1024]{2,1,0:T(1,128)S(1)} %broadcast_in_dim.48, f32[1,32,1024]{2,1,0:T(8,128)S(1)} %collective-permute-done, f32[16,32,1024]{2,1,0:T(8,128)} %bitcast.102, f32[1,32,1024]{2,1,0:T(8,128)} %copy-done.15, f32[34]{0:T(128)S(1)} %pad.74.clone), kind=kLoop, calls=%fused_computation.4 | loop fusion | flops 2506752 | bytes 4939912 | tf_op jit(solution)/shard_map/concatenate | solution.py:52
  14.6 7.1 %fusion.2 = f32[16,32,1024]{2,1,0:T(8,128)S(1)} fusion(f32[16,32,1024]{2,1,0:T(8,128)} %bitcast.103, f32[18,34,1024]{2,1,0:T(8,128)S(1)} %pad_maximum_fusion.3, f32[1,32,1024]{2,1,0:T(8,128)} %copy-done.14, f32[1,32,1024]{2,1,0:T(8,128)S(1)} %copy-done.16, f32[18,1,1024]{2,1,0:T(1,128)S(1)} %broadcast_in_dim.48, bf16[1,16,32,1024]{3,2,1,0:T(8,128)(2,1)S(1)} %copy-done.8, ...), kind=kLoop, calls=%fused_computation.35 | loop fusion | flops 18874368 | bytes 11231232 | tf_op jit(solution)/shard_map/add | solution.py:78
  21.7 1.3 copy-done.6
  23.0 0.7 fusion.61
  23.7 2.4 %collective-permute-start.2 = (f32[1,32,1024]{2,1,0:T(8,128)}, f32[1,32,1024]{2,1,0:T(8,128)}, u32[]{:S(2)}, u32[]{:S(2)}) collective-permute-start(f32[1,32,1024]{2,1,0:T(8,128)} %get-tuple-element.20), channel_id=1, source_target_pairs={{1,0},{2,1},{3,2},{4,3},{5,4},{6,5},{7,6},{9,8},{10,9},{11,10},{12... | collective-permute-start | bytes 393224 | tf_op jit(solution)/shard_map/ppermute | solution.py:22
  26.1 3.5 %collective-permute-start.3 = (f32[1,32,1024]{2,1,0:T(8,128)}, f32[1,32,1024]{2,1,0:T(8,128)}, u32[]{:S(2)}, u32[]{:S(2)}) collective-permute-start(f32[1,32,1024]{2,1,0:T(8,128)} %get-tuple-element.19), channel_id=1, source_target_pairs={{0,1},{1,2},{2,3},{3,4},{4,5},{5,6},{6,7},{8,9},{9,10},{10,11},{11... | collective-permute-start | bytes 393224 | tf_op jit(solution)/shard_map/ppermute | solution.py:20
  29.7 0.7 copy.21
  30.7 1.2 collective-permute-done.3
  31.9 2.2 %pad_maximum_fusion.2 = f32[18,34,1024]{2,1,0:T(8,128)S(1)} fusion(f32[18,1,1024]{2,1,0:T(1,128)S(1)} %broadcast_in_dim.48, f32[1,32,1024]{2,1,0:T(8,128)} %collective-permute-done.2, f32[16,32,1024]{2,1,0:T(8,128)} %copy-done.6, f32[1,32,1024]{2,1,0:T(8,128)} %collective-permute-done.3, f32[34]{0:T(128)S(1)} %pad.74.clone), kind=kLoop, calls=%fused_computation.3 | loop fusion | flops 2506752 | bytes 4939912 | tf_op jit(solution)/shard_map/concatenate | solution.py:52
  34.1 4.7 %fusion.5 = f32[16,32,1024]{2,1,0:T(8,128)S(1)} fusion(f32[16,32,1024]{2,1,0:T(8,128)S(1)} %copy-done.7, f32[18,34,1024]{2,1,0:T(8,128)S(1)} %pad_maximum_fusion.2, f32[1,32,1024]{2,1,0:T(8,128)} %collective-permute-done.2, f32[1,32,1024]{2,1,0:T(8,128)} %collective-permute-done.3, f32[18,1,1024]{2,1,0:T(1,128)S(1)} %broadcast_in_dim.48, ...), kind=kLoop, calls=%fused_computation.38 | loop fusion | flops 18874368 | bytes 11231232 | tf_op jit(solution)/shard_map/add | solution.py:78
  38.9 1.3 copy-done.4
  40.2 0.7 fusion.60
  40.9 1.9 %collective-permute-start.4 = (f32[1,32,1024]{2,1,0:T(8,128)}, f32[1,32,1024]{2,1,0:T(8,128)}, u32[]{:S(2)}, u32[]{:S(2)}) collective-permute-start(f32[1,32,1024]{2,1,0:T(8,128)} %get-tuple-element.18), channel_id=1, source_target_pairs={{1,0},{2,1},{3,2},{4,3},{5,4},{6,5},{7,6},{9,8},{10,9},{11,10},{12... | collective-permute-start | bytes 393224 | tf_op jit(solution)/shard_map/ppermute | solution.py:22
  42.8 4.4 %collective-permute-start.5 = (f32[1,32,1024]{2,1,0:T(8,128)}, f32[1,32,1024]{2,1,0:T(8,128)}, u32[]{:S(2)}, u32[]{:S(2)}) collective-permute-start(f32[1,32,1024]{2,1,0:T(8,128)} %get-tuple-element.17), channel_id=1, source_target_pairs={{0,1},{1,2},{2,3},{3,4},{4,5},{5,6},{6,7},{8,9},{9,10},{10,11},{11... | collective-permute-start | bytes 393224 | tf_op jit(solution)/shard_map/ppermute | solution.py:20
  47.2 0.9 fusion.37
  48.1 3.7 %all-to-all-start = ((f32[8,16,128]{2,1,0:T(8,128)}), f32[8,16,128]{2,1,0:T(8,128)S(1)}, u32[]{:S(2)}, u32[]{:S(2)}) async-start(f32[8,16,128]{2,1,0:T(8,128)} %fusion.37), calls=%async_computation | async-start | bytes 131072 | tf_op jit(solution)/shard_map/all_to_all | solution.py:44
  51.8 2.3 %pad_maximum_fusion.1 = f32[18,34,1024]{2,1,0:T(8,128)S(1)} fusion(f32[18,1,1024]{2,1,0:T(1,128)S(1)} %broadcast_in_dim.48, f32[1,32,1024]{2,1,0:T(8,128)} %collective-permute-done.4, f32[16,32,1024]{2,1,0:T(8,128)} %copy-done.4, f32[1,32,1024]{2,1,0:T(8,128)} %collective-permute-done.5, f32[34]{0:T(128)S(1)} %pad.74.clone), kind=kLoop, calls=%fused_computation.2 | loop fusion | flops 2506752 | bytes 4939912 | tf_op jit(solution)/shard_map/concatenate | solution.py:52
  54.4 4.7 %fusion.8 = f32[16,32,1024]{2,1,0:T(8,128)S(1)} fusion(f32[16,32,1024]{2,1,0:T(8,128)S(1)} %copy-done.5, f32[18,34,1024]{2,1,0:T(8,128)S(1)} %pad_maximum_fusion.1, f32[1,32,1024]{2,1,0:T(8,128)} %collective-permute-done.4, f32[1,32,1024]{2,1,0:T(8,128)} %collective-permute-done.5, f32[18,1,1024]{2,1,0:T(1,128)S(1)} %broadcast_in_dim.48, ...), kind=kLoop, calls=%fused_computation.41 | loop fusion | flops 18874368 | bytes 11231232 | tf_op jit(solution)/shard_map/add | solution.py:78
  59.1 1.3 copy-done.2
  60.4 0.7 fusion.59
  61.1 1.9 %collective-permute-start.6 = (f32[1,32,1024]{2,1,0:T(8,128)}, f32[1,32,1024]{2,1,0:T(8,128)}, u32[]{:S(2)}, u32[]{:S(2)}) collective-permute-start(f32[1,32,1024]{2,1,0:T(8,128)} %get-tuple-element.16), channel_id=1, source_target_pairs={{1,0},{2,1},{3,2},{4,3},{5,4},{6,5},{7,6},{9,8},{10,9},{11,10},{12... | collective-permute-start | bytes 393224 | tf_op jit(solution)/shard_map/ppermute | solution.py:22
  63.0 3.6 %collective-permute-start.7 = (f32[1,32,1024]{2,1,0:T(8,128)}, f32[1,32,1024]{2,1,0:T(8,128)}, u32[]{:S(2)}, u32[]{:S(2)}) collective-permute-start(f32[1,32,1024]{2,1,0:T(8,128)} %get-tuple-element.15), channel_id=1, source_target_pairs={{0,1},{1,2},{2,3},{3,4},{4,5},{5,6},{6,7},{8,9},{9,10},{10,11},{11... | collective-permute-start | bytes 393224 | tf_op jit(solution)/shard_map/ppermute | solution.py:20
  67.3 0.7 broadcast_in_dim.51
  68.0 11.3 %all-to-all-start.1 = ((f32[32,16,128]{2,1,0:T(8,128)}), f32[32,16,128]{2,1,0:T(8,128)}, u32[]{:S(2)}, u32[]{:S(2)}) async-start(f32[32,16,128]{2,1,0:T(8,128)} %broadcast_in_dim.51), calls=%async_computation.1 | async-start | bytes 524288 | tf_op jit(solution)/shard_map/all_to_all | solution.py:38
  79.4 2.3 %pad_maximum_fusion = f32[18,34,1024]{2,1,0:T(8,128)S(1)} fusion(f32[18,1,1024]{2,1,0:T(1,128)S(1)} %broadcast_in_dim.48, f32[1,32,1024]{2,1,0:T(8,128)} %collective-permute-done.6, f32[16,32,1024]{2,1,0:T(8,128)} %copy-done.2, f32[1,32,1024]{2,1,0:T(8,128)} %collective-permute-done.7, f32[34]{0:T(128)} %copy-done.20), kind=kLoop, calls=%fused_computation.1 | loop fusion | flops 2506752 | bytes 4939912 | tf_op jit(solution)/shard_map/concatenate | solution.py:52
  81.9 4.7 %fusion.11 = f32[16,32,1024]{2,1,0:T(8,128)S(1)} fusion(f32[16,32,1024]{2,1,0:T(8,128)S(1)} %copy-done.3, f32[18,34,1024]{2,1,0:T(8,128)S(1)} %pad_maximum_fusion, f32[1,32,1024]{2,1,0:T(8,128)} %collective-permute-done.6, f32[1,32,1024]{2,1,0:T(8,128)} %collective-permute-done.7, f32[18,1,1024]{2,1,0:T(1,128)S(1)} %broadcast_in_dim.48, ...), kind=kLoop, calls=%fused_computation.44 | loop fusion | flops 18874368 | bytes 11231232 | tf_op jit(solution)/shard_map/add | solution.py:78
  86.7 1.3 copy-done.12
  88.5 5.3 %collective-permute-start.8 = (f32[1,256]{1,0:T(1,128)S(1)}, f32[1,256]{1,0:T(1,128)S(1)}, u32[]{:S(2)}, u32[]{:S(2)}) collective-permute-start(f32[1,256]{1,0:T(1,128)S(1)} %div.18), channel_id=1, source_target_pairs={{0,128},{8,136},{16,144},{24,152},{32,160},{40,168},{48,176},{56,1... | collective-permute-start | bytes 3080 | tf_op jit(solution)/shard_map/ppermute | solution.py:32
  93.7 1.2 collective-permute-done.8
  95.0 11.7 %all_gather.3 = f32[1,2048]{1,0:T(1,128)S(1)} all-gather(f32[1,256]{1,0:T(1,128)S(1)} %collective-permute-done.8), channel_id=1, replica_groups=mesh['wide'=32,'slab'=8] {'slab'}, dimensions={1}, use_global_device_ids=true | all-gather | bytes 9216 | tf_op jit(solution)/shard_map/all_gather | solution.py:120
  106.6 1.7 %gather_fusion = f32[256]{0:T(256)S(1)} fusion(f32[2048]{0:T(1024)S(1)} %bitcast.101, s32[1024]{0:T(1024)S(1)} %pad_clamp_fusion), kind=kCustom, calls=%fused_computation | custom fusion | bytes 3072 | tf_op jit(solution)/shard_map/jit(_take)/gather | solution.py:121
  108.4 1.0 reduce_sum.38
  109.4 0.6 broadcast_in_dim.52
  110.0 3.4 %all-to-all-start.2 = ((f32[8,16,128]{2,1,0:T(8,128)}), f32[8,16,128]{2,1,0:T(8,128)S(1)}, u32[]{:S(2)}, u32[]{:S(2)}) async-start(f32[8,16,128]{2,1,0:T(8,128)} %broadcast_in_dim.52), calls=%async_computation.2 | async-start | bytes 131072 | tf_op jit(solution)/shard_map/all_to_all | solution.py:47
  113.6 4.7 %all-to-all-done.2 = f32[8,16,128]{2,1,0:T(8,128)S(1)} async-done(((f32[8,16,128]{2,1,0:T(8,128)}), f32[8,16,128]{2,1,0:T(8,128)S(1)}, u32[]{:S(2)}, u32[]{:S(2)}) %all-to-all-start.2) | async-done | bytes 65568 | tf_op jit(solution)/shard_map/all_to_all | solution.py:47
  118.3 0.7 broadcast_in_dim.54
  119.0 11.3 %all-to-all-start.3 = ((f32[256,1,128]{2,1,0:T(1,128)}), f32[256,1,128]{2,1,0:T(1,128)S(1)}, u32[]{:S(2)}, u32[]{:S(2)}) async-start(f32[256,1,128]{2,1,0:T(1,128)} %broadcast_in_dim.54), calls=%async_computation.3 | async-start | bytes 262144 | tf_op jit(solution)/shard_map/all_to_all | solution.py:38
  130.5 11.7 %cholesky.16 = f32[128,128]{1,0:T(8,128)S(1)} custom-call(f32[128,128]{1,0:T(8,128)S(1)} %fusion.45), custom_call_target="Cholesky" | custom-call | tf_op jit(solution)/shard_map/jit(cholesky)/cholesky | solution.py:128
  142.2 0.6 compare_reduce_fusion
  142.8 0.7 fusion.41
  143.5 9.8 %custom-call.10 = f32[1,128,128]{1,2,0:T(8,128)S(1)} custom-call(f32[1,128,128]{2,1,0:T(8,128)S(1)} %fusion.41), custom_call_target="InvertDiagBlocksLowerTriangular" | custom-call | tf_op jit(solution)/shard_map/triangular_solve | solution.py:132
  153.6 0.8 copy.25
  155.0 0.6 fusion.46
  (75 shorter events, 4.5 us)
Async XLA Ops:
  0.6 154.2 %copy-start = (f32[1,256,128]{2,1,0:T(8,128)S(1)}, f32[1,256,128]{2,1,0:T(8,128)}, u32[]{:S(2)}) copy-start(f32[1,256,128]{2,1,0:T(8,128)} %param.13) | copy-start | bytes 393220
  1.7 9.3 %collective-permute-start = (f32[1,32,1024]{2,1,0:T(8,128)S(1)}, f32[1,32,1024]{2,1,0:T(8,128)S(1)}, u32[]{:S(2)}, u32[]{:S(2)}) collective-permute-start(f32[1,32,1024]{2,1,0:T(8,128)S(1)} %get-tuple-element.22), channel_id=1, source_target_pairs={{1,0},{2,1},{3,2},{4,3},{5,4},{6,5},{7,6},{9,8},{10,9},{11,10},{12... | collective-permute-start | bytes 393224 | tf_op jit(solution)/shard_map/ppermute | solution.py:22
  6.8 4.2 %collective-permute-start.1 = (f32[1,32,1024]{2,1,0:T(8,128)S(1)}, f32[1,32,1024]{2,1,0:T(8,128)S(1)}, u32[]{:S(2)}, u32[]{:S(2)}) collective-permute-start(f32[1,32,1024]{2,1,0:T(8,128)S(1)} %get-tuple-element.21), channel_id=1, source_target_pairs={{0,1},{1,2},{2,3},{3,4},{4,5},{5,6},{6,7},{8,9},{9,10},{10,11},{11... | collective-permute-start | bytes 393224 | tf_op jit(solution)/shard_map/ppermute | solution.py:20
  11.0 40.8 %copy-start.20 = (f32[34]{0:T(128)}, f32[34]{0:T(128)S(1)}, u32[]{:S(2)}) copy-start(f32[34]{0:T(128)S(1)} %pad.74.clone) | copy-start | bytes 412
  11.0 0.7 copy-start.14
  11.0 0.7 copy-start.15
  11.7 2.6 %copy-start.1 = (bf16[3,1,16,32,1024]{4,3,2,1,0:T(8,128)(2,1)S(1)}, bf16[3,1,16,32,1024]{4,3,2,1,0:T(8,128)(2,1)}, u32[]{:S(2)}) copy-start(bf16[3,1,16,32,1024]{4,3,2,1,0:T(8,128)(2,1)} %param.9) | copy-start | bytes 9437188
  11.7 2.8 %copy-start.8 = (bf16[1,16,32,1024]{3,2,1,0:T(8,128)(2,1)S(1)}, bf16[1,16,32,1024]{3,2,1,0:T(8,128)(2,1)}, u32[]{:S(2)}) copy-start(bf16[1,16,32,1024]{3,2,1,0:T(8,128)(2,1)} %param.8) | copy-start | bytes 3145732
  11.7 2.8 %copy-start.16 = (f32[1,32,1024]{2,1,0:T(8,128)S(1)}, f32[1,32,1024]{2,1,0:T(8,128)}, u32[]{:S(2)}) copy-start(f32[1,32,1024]{2,1,0:T(8,128)} %copy-done.15) | copy-start | bytes 393220
  14.6 15.1 %copy-start.13 = (f32[1,256,128]{2,1,0:T(8,128)S(1)}, f32[1,256,128]{2,1,0:T(8,128)}, u32[]{:S(2)}) copy-start(f32[1,256,128]{2,1,0:T(8,128)} %param.12) | copy-start | bytes 393220
  21.7 1.3 copy-start.6
  23.7 6.9 %collective-permute-start.2 = (f32[1,32,1024]{2,1,0:T(8,128)}, f32[1,32,1024]{2,1,0:T(8,128)}, u32[]{:S(2)}, u32[]{:S(2)}) collective-permute-start(f32[1,32,1024]{2,1,0:T(8,128)} %get-tuple-element.20), channel_id=1, source_target_pairs={{1,0},{2,1},{3,2},{4,3},{5,4},{6,5},{7,6},{9,8},{10,9},{11,10},{12... | collective-permute-start | bytes 393224 | tf_op jit(solution)/shard_map/ppermute | solution.py:22
  26.1 5.7 %collective-permute-start.3 = (f32[1,32,1024]{2,1,0:T(8,128)}, f32[1,32,1024]{2,1,0:T(8,128)}, u32[]{:S(2)}, u32[]{:S(2)}) collective-permute-start(f32[1,32,1024]{2,1,0:T(8,128)} %get-tuple-element.19), channel_id=1, source_target_pairs={{0,1},{1,2},{2,3},{3,4},{4,5},{5,6},{6,7},{8,9},{9,10},{10,11},{11... | collective-permute-start | bytes 393224 | tf_op jit(solution)/shard_map/ppermute | solution.py:20
  30.4 3.7 %copy-start.7 = (f32[16,32,1024]{2,1,0:T(8,128)S(1)}, f32[16,32,1024]{2,1,0:T(8,128)}, u32[]{:S(2)}) copy-start(f32[16,32,1024]{2,1,0:T(8,128)} %copy-done.6) | copy-start | bytes 6291460
  30.4 3.7 %copy-start.9 = (bf16[1,16,32,1024]{3,2,1,0:T(8,128)(2,1)S(1)}, bf16[1,16,32,1024]{3,2,1,0:T(8,128)(2,1)}, u32[]{:S(2)}) copy-start(bf16[1,16,32,1024]{3,2,1,0:T(8,128)(2,1)} %param.8) | copy-start | bytes 3145732
  34.1 13.1 %copy-start.17 = (f32[1,256,128]{1,2,0:T(8,128)S(1)}, f32[1,256,128]{1,2,0:T(8,128)}, u32[]{:S(2)}) copy-start(f32[1,256,128]{1,2,0:T(8,128)} %copy.21) | copy-start | bytes 393220
  38.8 1.3 copy-start.4
  40.9 10.9 %collective-permute-start.4 = (f32[1,32,1024]{2,1,0:T(8,128)}, f32[1,32,1024]{2,1,0:T(8,128)}, u32[]{:S(2)}, u32[]{:S(2)}) collective-permute-start(f32[1,32,1024]{2,1,0:T(8,128)} %get-tuple-element.18), channel_id=1, source_target_pairs={{1,0},{2,1},{3,2},{4,3},{5,4},{6,5},{7,6},{9,8},{10,9},{11,10},{12... | collective-permute-start | bytes 393224 | tf_op jit(solution)/shard_map/ppermute | solution.py:22
  42.8 9.0 %collective-permute-start.5 = (f32[1,32,1024]{2,1,0:T(8,128)}, f32[1,32,1024]{2,1,0:T(8,128)}, u32[]{:S(2)}, u32[]{:S(2)}) collective-permute-start(f32[1,32,1024]{2,1,0:T(8,128)} %get-tuple-element.17), channel_id=1, source_target_pairs={{0,1},{1,2},{2,3},{3,4},{4,5},{5,6},{6,7},{8,9},{9,10},{10,11},{11... | collective-permute-start | bytes 393224 | tf_op jit(solution)/shard_map/ppermute | solution.py:20
  48.1 19.2 %all-to-all-start = ((f32[8,16,128]{2,1,0:T(8,128)}), f32[8,16,128]{2,1,0:T(8,128)S(1)}, u32[]{:S(2)}, u32[]{:S(2)}) async-start(f32[8,16,128]{2,1,0:T(8,128)} %fusion.37), calls=%async_computation | async-start | bytes 131072 | tf_op jit(solution)/shard_map/all_to_all | solution.py:44
  51.8 2.4 %copy-start.5 = (f32[16,32,1024]{2,1,0:T(8,128)S(1)}, f32[16,32,1024]{2,1,0:T(8,128)}, u32[]{:S(2)}) copy-start(f32[16,32,1024]{2,1,0:T(8,128)} %copy-done.4) | copy-start | bytes 6291460
  51.8 2.6 %copy-start.10 = (bf16[1,16,32,1024]{3,2,1,0:T(8,128)(2,1)S(1)}, bf16[1,16,32,1024]{3,2,1,0:T(8,128)(2,1)}, u32[]{:S(2)}) copy-start(bf16[1,16,32,1024]{3,2,1,0:T(8,128)(2,1)} %param.8) | copy-start | bytes 3145732
  54.4 12.3 %copy-start.18 = (s32[1,256]{1,0:T(1,128)S(1)}, s32[1,256]{1,0:T(1,128)}, u32[]{:S(2)}) copy-start(s32[1,256]{1,0:T(1,128)} %param.11) | copy-start | bytes 3076
  59.1 1.3 copy-start.2
  61.1 18.2 %collective-permute-start.6 = (f32[1,32,1024]{2,1,0:T(8,128)}, f32[1,32,1024]{2,1,0:T(8,128)}, u32[]{:S(2)}, u32[]{:S(2)}) collective-permute-start(f32[1,32,1024]{2,1,0:T(8,128)} %get-tuple-element.16), channel_id=1, source_target_pairs={{1,0},{2,1},{3,2},{4,3},{5,4},{6,5},{7,6},{9,8},{10,9},{11,10},{12... | collective-permute-start | bytes 393224 | tf_op jit(solution)/shard_map/ppermute | solution.py:22
  63.0 16.3 %collective-permute-start.7 = (f32[1,32,1024]{2,1,0:T(8,128)}, f32[1,32,1024]{2,1,0:T(8,128)}, u32[]{:S(2)}, u32[]{:S(2)}) collective-permute-start(f32[1,32,1024]{2,1,0:T(8,128)} %get-tuple-element.15), channel_id=1, source_target_pairs={{0,1},{1,2},{2,3},{3,4},{4,5},{5,6},{6,7},{8,9},{9,10},{10,11},{11... | collective-permute-start | bytes 393224 | tf_op jit(solution)/shard_map/ppermute | solution.py:20
  68.0 40.4 %all-to-all-start.1 = ((f32[32,16,128]{2,1,0:T(8,128)}), f32[32,16,128]{2,1,0:T(8,128)}, u32[]{:S(2)}, u32[]{:S(2)}) async-start(f32[32,16,128]{2,1,0:T(8,128)} %broadcast_in_dim.51), calls=%async_computation.1 | async-start | bytes 524288 | tf_op jit(solution)/shard_map/all_to_all | solution.py:38
  79.3 2.4 %copy-start.3 = (f32[16,32,1024]{2,1,0:T(8,128)S(1)}, f32[16,32,1024]{2,1,0:T(8,128)}, u32[]{:S(2)}) copy-start(f32[16,32,1024]{2,1,0:T(8,128)} %copy-done.2) | copy-start | bytes 6291460
  79.4 2.6 %copy-start.11 = (bf16[1,16,32,1024]{3,2,1,0:T(8,128)(2,1)S(1)}, bf16[1,16,32,1024]{3,2,1,0:T(8,128)(2,1)}, u32[]{:S(2)}) copy-start(bf16[1,16,32,1024]{3,2,1,0:T(8,128)(2,1)} %param.8) | copy-start | bytes 3145732
  81.9 11.8 %copy-start.22 = (s32[256,1]{0,1:T(1,128)S(1)}, s32[256,1]{0,1:T(1,128)}, u32[]{:S(2)}) copy-start(s32[256,1]{0,1:T(1,128)} %compare_select_fusion.1) | copy-start | bytes 3076
  81.9 31.5 %copy-start.19 = (s32[1,256]{1,0:T(1,128)S(1)}, s32[1,256]{1,0:T(1,128)}, u32[]{:S(2)}) copy-start(s32[1,256]{1,0:T(1,128)} %param.11) | copy-start | bytes 3076
  81.9 31.5 %copy-start.21 = (f32[1,256]{1,0:T(1,128)S(1)}, f32[1,256]{1,0:T(1,128)}, u32[]{:S(2)}) copy-start(f32[1,256]{1,0:T(1,128)} %param.10) | copy-start | bytes 3076
  86.7 1.3 copy-start.12
  88.5 6.5 %collective-permute-start.8 = (f32[1,256]{1,0:T(1,128)S(1)}, f32[1,256]{1,0:T(1,128)S(1)}, u32[]{:S(2)}, u32[]{:S(2)}) collective-permute-start(f32[1,256]{1,0:T(1,128)S(1)} %div.18), channel_id=1, source_target_pairs={{0,128},{8,136},{16,144},{24,152},{32,160},{40,168},{48,176},{56,1... | collective-permute-start | bytes 3080 | tf_op jit(solution)/shard_map/ppermute | solution.py:32
  110.0 8.3 %all-to-all-start.2 = ((f32[8,16,128]{2,1,0:T(8,128)}), f32[8,16,128]{2,1,0:T(8,128)S(1)}, u32[]{:S(2)}, u32[]{:S(2)}) async-start(f32[8,16,128]{2,1,0:T(8,128)} %broadcast_in_dim.52), calls=%async_computation.2 | async-start | bytes 131072 | tf_op jit(solution)/shard_map/all_to_all | solution.py:47
  119.0 35.4 %all-to-all-start.3 = ((f32[256,1,128]{2,1,0:T(1,128)}), f32[256,1,128]{2,1,0:T(1,128)S(1)}, u32[]{:S(2)}, u32[]{:S(2)}) async-start(f32[256,1,128]{2,1,0:T(1,128)} %broadcast_in_dim.54), calls=%async_computation.3 | async-start | bytes 262144 | tf_op jit(solution)/shard_map/all_to_all | solution.py:38
where the time goes:
time: 156 us
  starting transfers between devices  59.9 us (38%)
  other arithmetic  56.9 us (36%)
  local copies, waits for them, and re-layouts  16.7 us (11%)
  blocking collectives  11.7 us (8%)
  waiting for transfers between devices  7.42 us (5%)
  matrix products  1.95 us (1%)
    all_to_all x2, starting transfers between devices, gather_sum(): return jnp.sum(lax.all_to_all(copies, axes, 0, 0, tiled=True), axis=0)  22.6 us
    add x4, other arithmetic, march_forward(): centre + STEP_SIZE * (diffuse_subdomain.astype(jnp.float32) * spread - ca...  21.2 us
    ppermute x4, starting transfers between devices, padded(): lax.ppermute(tail, axis, [(i, (i + 1) % count) for i in range(ends)])  13.4 us
    another operation x3, other arithmetic, shards(): lower_factor = jnp.linalg.cholesky(gram_matrix)  12.4 us
    all_gather x1, blocking collectives, shards(): partner_all = lax.all_gather(partner_own, 'slab', axis=1, tiled=True)  11.7 us
    ppermute x4, starting transfers between devices, padded(): lax.ppermute(head, axis, [((i + 1) % count, i) for i in range(ends)])  11.4 us
    another operation x2, other arithmetic, shards(): lax.linalg.triangular_solve(lower_factor, half_solve, left_side=True, low...  10.5 us
    concatenate x4, other arithmetic, surround_wrapper(): jnp.concatenate([bottom, block_rows, mirror_layer[:, None, :]], axis=1)  9.12 us
  transfers between devices with their start and end apart: 13, of which 4 were waited for; matrix products, arithmetic and copies ran while one was open for 30% of the time, Pallas kernels for 0%

commit v1 on v0

--- a/solution.py
+++ b/solution.py
@@ -7,6 +7,12 @@
 INTERFACE_STRIP = 64
 SWEEPS = 4
 STEP_SIZE = 0.11
+
+
+def measure_samples_all_up(payload):
+    return jnp.concatenate(
+        lax.all_to_all(jnp.stack([payload for _ in range(lax.axis_size("slab"))]), "slab", 0, 0), 1
+    )
 
 
 def padded(cells, sides, width):
@@ -117,7 +123,7 @@
     face_means = face_means.reshape(1, rows_dev)
     top_bit = lax.axis_size("wide").bit_length() - 2
     partner_own = partner(face_means, "wide", top_bit)
-    partner_all = lax.all_gather(partner_own, "slab", axis=1, tiled=True)
+    partner_all = measure_samples_all_up(partner_own)
     tilde = jnp.take(partner_all[0], partner_facing_rows[0], axis=0)
     resid = tilde - interface_guess[0]
     proj_local = jnp.dot(

time: 156 us -> 160 us (1.026)
  waiting for transfers between devices: 7.42 us -> 23.1 us
  blocking collectives: 11.7 us -> 0 us
  starting transfers between devices: 59.9 us -> 63.3 us
  other arithmetic: 56.9 us -> 54.3 us
    all_gather x1 -> x0, blocking collectives: 11.7 us -> none  [shards(): partner_all = lax.all_gather(partner_own, 'slab', axis=1, tiled=True)]
    all_to_all x2, waiting for transfers between devices: 0.01 us -> 9.44 us  [gather_sum(): return jnp.sum(lax.all_to_all(copies, axes, 0, 0, tiled=True), axis=0)]
    all_to_all x2, starting transfers between devices: 22.6 us -> 15.7 us  [gather_sum(): return jnp.sum(lax.all_to_all(copies, axes, 0, 0, tiled=True), axis=0)]
    all_to_all x0 -> x1, starting transfers between devices: none -> 5.67 us  [measure_samples_all_up(): lax.all_to_all(jnp.stack([payload for _ in range(lax.axis_size('slab'))])...]
    all_to_all x0 -> x1, waiting for transfers between devices: none -> 4.6 us  [measure_samples_all_up(): lax.all_to_all(jnp.stack([payload for _ in range(lax.axis_size('slab'))])...]
    all_to_all x1, starting transfers between devices: 3.44 us -> 5.69 us  [sum_everywhere(): lax.all_to_all(copies, 'slab', 0, 0, tiled=True).reshape(square.shape)]
    concatenate x4, other arithmetic: 9.12 us -> 7.44 us  [surround_wrapper(): jnp.concatenate([bottom, block_rows, mirror_layer[:, None, :]], axis=1)]
    ppermute x1, starting transfers between devices: 5.28 us -> 6.94 us  [partner(): return lax.ppermute(value, axis, pairs)]
  transfers between devices with their start and end apart: 13 -> 14, of which waited for: 4 -> 8; matrix products, arithmetic and copies ran while one was open for 30% -> 23% of each run, Pallas kernels for 0% -> 0%
where the time goes in v1:
time: 160 us; the launch traced here: 159 us
  starting transfers between devices  63.3 us (40%)
  other arithmetic  54.3 us (34%)
  waiting for transfers between devices  23.1 us (14%)
  local copies, waits for them, and re-layouts  15.1 us (9%)
  matrix products  1.95 us (1%)
    add x4, other arithmetic, march_forward(): centre + STEP_SIZE * (diffuse_subdomain.astype(jnp.float32) * spread - ca...  21.8 us
    all_to_all x2, starting transfers between devices, gather_sum(): return jnp.sum(lax.all_to_all(copies, axes, 0, 0, tiled=True), axis=0)  15.7 us
    ppermute x4, starting transfers between devices, padded(): lax.ppermute(tail, axis, [(i, (i + 1) % count) for i in range(ends)])  14.2 us
    another operation x3, other arithmetic, shards(): lower_factor = jnp.linalg.cholesky(gram_matrix)  12.4 us
    ppermute x4, starting transfers between devices, padded(): lax.ppermute(head, axis, [((i + 1) % count, i) for i in range(ends)])  11.4 us
    another operation x2, other arithmetic, shards(): lax.linalg.triangular_solve(lower_factor, half_solve, left_side=True, low...  10.5 us
    all_to_all x2, waiting for transfers between devices, gather_sum(): return jnp.sum(lax.all_to_all(copies, axes, 0, 0, tiled=True), axis=0)  9.44 us
    unnamed x35, local copies, waits for them, and re-layouts  7.45 us
  transfers between devices with their start and end apart: 14, of which 8 were waited for; matrix products, arithmetic and copies ran while one was open for 23% of the time, Pallas kernels for 0%

profile of v1, /device:TPU:1, one launch (start us, length us, event | category | flops | bytes accessed | tf_op | source)
XLA Modules:
  0.0 158.8 jit_solution(14438123083305958050)
XLA Ops:
  0.6 1.0 slice_bitcast_fusion
  1.7 5.1 %collective-permute-start = (f32[1,32,1024]{2,1,0:T(8,128)S(1)}, f32[1,32,1024]{2,1,0:T(8,128)S(1)}, u32[]{:S(2)}, u32[]{:S(2)}) collective-permute-start(f32[1,32,1024]{2,1,0:T(8,128)S(1)} %get-tuple-element.22), channel_id=1, source_target_pairs={{1,0},{2,1},{3,2},{4,3},{5,4},{6,5},{7,6},{9,8},{10,9},{11,10},{12... | collective-permute-start | bytes 393224 | tf_op jit(solution)/shard_map/ppermute | solution.py:28
  6.8 1.9 %collective-permute-start.1 = (f32[1,32,1024]{2,1,0:T(8,128)S(1)}, f32[1,32,1024]{2,1,0:T(8,128)S(1)}, u32[]{:S(2)}, u32[]{:S(2)}) collective-permute-start(f32[1,32,1024]{2,1,0:T(8,128)S(1)} %get-tuple-element.21), channel_id=1, source_target_pairs={{0,1},{1,2},{2,3},{3,4},{4,5},{5,6},{6,7},{8,9},{9,10},{10,11},{11... | collective-permute-start | bytes 393224 | tf_op jit(solution)/shard_map/ppermute | solution.py:26
  9.3 1.3 reduce.12
  11.0 0.6 copy-done.11
  11.7 2.3 %pad_maximum_fusion.3 = f32[18,34,1024]{2,1,0:T(8,128)S(1)} fusion(f32[18,1,1024]{2,1,0:T(1,128)S(1)} %broadcast_in_dim.48, f32[1,32,1024]{2,1,0:T(8,128)S(1)} %collective-permute-done, f32[16,32,1024]{2,1,0:T(8,128)} %bitcast.103, f32[1,32,1024]{2,1,0:T(8,128)} %copy-done.11, f32[34]{0:T(128)S(1)} %pad.74.clone), kind=kLoop, calls=%fused_computation.4 | loop fusion | flops 2506752 | bytes 4939912 | tf_op jit(solution)/shard_map/concatenate | solution.py:58
  14.5 7.0 %fusion.2 = f32[16,32,1024]{2,1,0:T(8,128)S(1)} fusion(f32[16,32,1024]{2,1,0:T(8,128)} %bitcast.104, f32[18,34,1024]{2,1,0:T(8,128)S(1)} %pad_maximum_fusion.3, f32[1,32,1024]{2,1,0:T(8,128)S(1)} %collective-permute-done, f32[1,32,1024]{2,1,0:T(8,128)S(1)} %copy-done.12, f32[18,1,1024]{2,1,0:T(1,128)S(1)} %broadcast_in_dim.48, ...), kind=kLoop, calls=%fused_computation.35 | loop fusion | flops 18874368 | bytes 11231232 | tf_op jit(solution)/shard_map/add | solution.py:84
  21.5 2.4 %collective-permute-start.2 = (f32[1,32,1024]{2,1,0:T(8,128)S(1)}, f32[1,32,1024]{2,1,0:T(8,128)S(1)}, u32[]{:S(2)}, u32[]{:S(2)}) collective-permute-start(f32[1,32,1024]{2,1,0:T(8,128)S(1)} %get-tuple-element.20), channel_id=1, source_target_pairs={{1,0},{2,1},{3,2},{4,3},{5,4},{6,5},{7,6},{9,8},{10,9},{11,10},{12... | collective-permute-start | bytes 393224 | tf_op jit(solution)/shard_map/ppermute | solution.py:28
  24.0 3.5 %collective-permute-start.3 = (f32[1,32,1024]{2,1,0:T(8,128)S(1)}, f32[1,32,1024]{2,1,0:T(8,128)S(1)}, u32[]{:S(2)}, u32[]{:S(2)}) collective-permute-start(f32[1,32,1024]{2,1,0:T(8,128)S(1)} %get-tuple-element.19), channel_id=1, source_target_pairs={{0,1},{1,2},{2,3},{3,4},{4,5},{5,6},{6,7},{8,9},{9,10},{10,11},{11... | collective-permute-start | bytes 393224 | tf_op jit(solution)/shard_map/ppermute | solution.py:26
  27.5 0.7 collective-permute-done.2
  28.2 1.2 collective-permute-done.3
  29.4 0.7 pad_maximum_fusion.2
  30.1 5.4 %fusion.5 = f32[16,32,1024]{2,1,0:T(8,128)S(1)} fusion(f32[16,32,1024]{2,1,0:T(8,128)S(1)} %fusion.2, f32[18,34,1024]{2,1,0:T(8,128)S(1)} %pad_maximum_fusion.2, f32[1,32,1024]{2,1,0:T(8,128)S(1)} %collective-permute-done.2, f32[1,32,1024]{2,1,0:T(8,128)S(1)} %collective-permute-done.3, f32[18,1,1024]{2,1,0:T(1,128)S(1)} %broadcast_in_dim.48, ...), kind=kLoop, calls=%fused_computation.38 | loop fusion | flops 18874368 | bytes 11231232 | tf_op jit(solution)/shard_map/add | solution.py:84
  35.5 1.3 copy-done.4
  36.8 0.7 fusion.60
  37.6 1.9 %collective-permute-start.4 = (f32[1,32,1024]{2,1,0:T(8,128)}, f32[1,32,1024]{2,1,0:T(8,128)}, u32[]{:S(2)}, u32[]{:S(2)}) collective-permute-start(f32[1,32,1024]{2,1,0:T(8,128)} %get-tuple-element.18), channel_id=1, source_target_pairs={{1,0},{2,1},{3,2},{4,3},{5,4},{6,5},{7,6},{9,8},{10,9},{11,10},{12... | collective-permute-start | bytes 393224 | tf_op jit(solution)/shard_map/ppermute | solution.py:28
  39.5 4.4 %collective-permute-start.5 = (f32[1,32,1024]{2,1,0:T(8,128)}, f32[1,32,1024]{2,1,0:T(8,128)}, u32[]{:S(2)}, u32[]{:S(2)}) collective-permute-start(f32[1,32,1024]{2,1,0:T(8,128)} %get-tuple-element.17), channel_id=1, source_target_pairs={{0,1},{1,2},{2,3},{3,4},{4,5},{5,6},{6,7},{8,9},{9,10},{10,11},{11... | collective-permute-start | bytes 393224 | tf_op jit(solution)/shard_map/ppermute | solution.py:26
  43.9 0.8 copy.21
  44.9 1.2 collective-permute-done.5
  46.1 2.2 %pad_maximum_fusion.1 = f32[18,34,1024]{2,1,0:T(8,128)S(1)} fusion(f32[18,1,1024]{2,1,0:T(1,128)S(1)} %broadcast_in_dim.48, f32[1,32,1024]{2,1,0:T(8,128)} %collective-permute-done.4, f32[16,32,1024]{2,1,0:T(8,128)} %copy-done.4, f32[1,32,1024]{2,1,0:T(8,128)} %collective-permute-done.5, f32[34]{0:T(128)S(1)} %pad.74.clone), kind=kLoop, calls=%fused_computation.2 | loop fusion | flops 2506752 | bytes 4939912 | tf_op jit(solution)/shard_map/concatenate | solution.py:58
  48.3 4.7 %fusion.8 = f32[16,32,1024]{2,1,0:T(8,128)S(1)} fusion(f32[16,32,1024]{2,1,0:T(8,128)S(1)} %copy-done.5, f32[18,34,1024]{2,1,0:T(8,128)S(1)} %pad_maximum_fusion.1, f32[1,32,1024]{2,1,0:T(8,128)} %collective-permute-done.4, f32[1,32,1024]{2,1,0:T(8,128)} %collective-permute-done.5, f32[18,1,1024]{2,1,0:T(1,128)S(1)} %broadcast_in_dim.48, ...), kind=kLoop, calls=%fused_computation.41 | loop fusion | flops 18874368 | bytes 11231232 | tf_op jit(solution)/shard_map/add | solution.py:84
  53.1 1.3 copy-done.2
  54.4 0.7 fusion.59
  55.1 1.9 %collective-permute-start.6 = (f32[1,32,1024]{2,1,0:T(8,128)}, f32[1,32,1024]{2,1,0:T(8,128)}, u32[]{:S(2)}, u32[]{:S(2)}) collective-permute-start(f32[1,32,1024]{2,1,0:T(8,128)} %get-tuple-element.16), channel_id=1, source_target_pairs={{1,0},{2,1},{3,2},{4,3},{5,4},{6,5},{7,6},{9,8},{10,9},{11,10},{12... | collective-permute-start | bytes 393224 | tf_op jit(solution)/shard_map/ppermute | solution.py:28
  57.0 4.4 %collective-permute-start.7 = (f32[1,32,1024]{2,1,0:T(8,128)}, f32[1,32,1024]{2,1,0:T(8,128)}, u32[]{:S(2)}, u32[]{:S(2)}) collective-permute-start(f32[1,32,1024]{2,1,0:T(8,128)} %get-tuple-element.15), channel_id=1, source_target_pairs={{0,1},{1,2},{2,3},{3,4},{4,5},{5,6},{6,7},{8,9},{9,10},{10,11},{11... | collective-permute-start | bytes 393224 | tf_op jit(solution)/shard_map/ppermute | solution.py:26
  61.4 0.9 fusion.37
  62.3 3.7 %all-to-all-start.1 = ((f32[8,16,128]{2,1,0:T(8,128)}), f32[8,16,128]{2,1,0:T(8,128)S(1)}, u32[]{:S(2)}, u32[]{:S(2)}) async-start(f32[8,16,128]{2,1,0:T(8,128)} %fusion.37), calls=%async_computation.1 | async-start | bytes 131072 | tf_op jit(solution)/shard_map/all_to_all | solution.py:50
  66.0 2.3 %pad_maximum_fusion = f32[18,34,1024]{2,1,0:T(8,128)S(1)} fusion(f32[18,1,1024]{2,1,0:T(1,128)S(1)} %broadcast_in_dim.48, f32[1,32,1024]{2,1,0:T(8,128)} %collective-permute-done.6, f32[16,32,1024]{2,1,0:T(8,128)} %copy-done.2, f32[1,32,1024]{2,1,0:T(8,128)} %collective-permute-done.7, f32[34]{0:T(128)S(1)} %pad.74.clone), kind=kLoop, calls=%fused_computation.1 | loop fusion | flops 2506752 | bytes 4939912 | tf_op jit(solution)/shard_map/concatenate | solution.py:58
  68.6 4.7 %fusion.11 = f32[16,32,1024]{2,1,0:T(8,128)S(1)} fusion(f32[16,32,1024]{2,1,0:T(8,128)S(1)} %copy-done.3, f32[18,34,1024]{2,1,0:T(8,128)S(1)} %pad_maximum_fusion, f32[1,32,1024]{2,1,0:T(8,128)} %collective-permute-done.6, f32[1,32,1024]{2,1,0:T(8,128)} %collective-permute-done.7, f32[18,1,1024]{2,1,0:T(1,128)S(1)} %broadcast_in_dim.48, ...), kind=kLoop, calls=%fused_computation.44 | loop fusion | flops 18874368 | bytes 11231232 | tf_op jit(solution)/shard_map/add | solution.py:84
  73.3 1.3 copy-done.9
  75.1 6.9 %collective-permute-start.8 = (f32[1,256]{1,0:T(1,128)S(1)}, f32[1,256]{1,0:T(1,128)S(1)}, u32[]{:S(2)}, u32[]{:S(2)}) collective-permute-start(f32[1,256]{1,0:T(1,128)S(1)} %div.18), channel_id=1, source_target_pairs={{0,128},{8,136},{16,144},{24,152},{32,160},{40,168},{48,176},{56,1... | collective-permute-start | bytes 3080 | tf_op jit(solution)/shard_map/ppermute | solution.py:38
  82.0 1.0 collective-permute-done.8
  83.6 5.7 %all-to-all-start = ((f32[8,1,256]{2,1,0:T(1,128)}), f32[8,1,256]{2,1,0:T(1,128)S(1)}, u32[]{:S(2)}, u32[]{:S(2)}) async-start(f32[8,1,256]{2,1,0:T(1,128)} %stack.2), calls=%async_computation | async-start | bytes 16384 | tf_op jit(solution)/shard_map/all_to_all | solution.py:14
  89.3 4.6 %all-to-all-done = f32[8,1,256]{2,1,0:T(1,128)S(1)} async-done(((f32[8,1,256]{2,1,0:T(1,128)}), f32[8,1,256]{2,1,0:T(1,128)S(1)}, u32[]{:S(2)}, u32[]{:S(2)}) %all-to-all-start) | async-done | bytes 8224 | tf_op jit(solution)/shard_map/all_to_all | solution.py:14
  93.9 0.7 broadcast_in_dim.51
  94.6 9.9 %all-to-all-start.2 = ((f32[32,16,128]{2,1,0:T(8,128)}), f32[32,16,128]{2,1,0:T(8,128)S(1)}, u32[]{:S(2)}, u32[]{:S(2)}) async-start(f32[32,16,128]{2,1,0:T(8,128)} %broadcast_in_dim.51), calls=%async_computation.2 | async-start | bytes 524288 | tf_op jit(solution)/shard_map/all_to_all | solution.py:44
  104.6 1.7 %gather_fusion = f32[256]{0:T(256)S(1)} fusion(f32[2048]{0:T(1024)S(1)} %bitcast.102, s32[1024]{0:T(1024)S(1)} %pad_clamp_fusion), kind=kCustom, calls=%fused_computation | custom fusion | bytes 3072 | tf_op jit(solution)/shard_map/jit(_take)/gather | solution.py:127
  106.3 9.4 %all-to-all-done.2 = f32[32,16,128]{2,1,0:T(8,128)S(1)} async-done(((f32[32,16,128]{2,1,0:T(8,128)}), f32[32,16,128]{2,1,0:T(8,128)S(1)}, u32[]{:S(2)}, u32[]{:S(2)}) %all-to-all-start.2) | async-done | bytes 262176 | tf_op jit(solution)/shard_map/all_to_all | solution.py:44
  115.8 0.6 broadcast_in_dim.52
  116.4 5.7 %all-to-all-start.3 = ((f32[8,16,128]{2,1,0:T(8,128)}), f32[8,16,128]{2,1,0:T(8,128)S(1)}, u32[]{:S(2)}, u32[]{:S(2)}) async-start(f32[8,16,128]{2,1,0:T(8,128)} %broadcast_in_dim.52), calls=%async_computation.3 | async-start | bytes 131072 | tf_op jit(solution)/shard_map/all_to_all | solution.py:53
  122.3 4.7 %all-to-all-done.3 = f32[8,16,128]{2,1,0:T(8,128)S(1)} async-done(((f32[8,16,128]{2,1,0:T(8,128)}), f32[8,16,128]{2,1,0:T(8,128)S(1)}, u32[]{:S(2)}, u32[]{:S(2)}) %all-to-all-start.3) | async-done | bytes 65568 | tf_op jit(solution)/shard_map/all_to_all | solution.py:53
  127.0 0.7 broadcast_in_dim.54
  127.7 5.8 %all-to-all-start.4 = ((f32[256,1,128]{2,1,0:T(1,128)}), f32[256,1,128]{2,1,0:T(1,128)S(1)}, u32[]{:S(2)}, u32[]{:S(2)}) async-start(f32[256,1,128]{2,1,0:T(1,128)} %broadcast_in_dim.54), calls=%async_computation.4 | async-start | bytes 262144 | tf_op jit(solution)/shard_map/all_to_all | solution.py:44
  133.6 11.7 %cholesky.16 = f32[128,128]{1,0:T(8,128)S(1)} custom-call(f32[128,128]{1,0:T(8,128)S(1)} %fusion.45), custom_call_target="Cholesky" | custom-call | tf_op jit(solution)/shard_map/jit(cholesky)/cholesky | solution.py:134
  145.4 0.6 compare_reduce_fusion
  146.0 0.7 fusion.41
  146.7 9.8 %custom-call.10 = f32[1,128,128]{1,2,0:T(8,128)S(1)} custom-call(f32[1,128,128]{2,1,0:T(8,128)S(1)} %fusion.41), custom_call_target="InvertDiagBlocksLowerTriangular" | custom-call | tf_op jit(solution)/shard_map/triangular_solve | solution.py:138
  156.8 0.8 copy.25
  (63 shorter events, 5.0 us)
Async XLA Ops:
  0.6 157.3 %copy-start = (f32[1,256,128]{2,1,0:T(8,128)S(1)}, f32[1,256,128]{2,1,0:T(8,128)}, u32[]{:S(2)}) copy-start(f32[1,256,128]{2,1,0:T(8,128)} %param.13) | copy-start | bytes 393220
  1.7 9.3 %collective-permute-start = (f32[1,32,1024]{2,1,0:T(8,128)S(1)}, f32[1,32,1024]{2,1,0:T(8,128)S(1)}, u32[]{:S(2)}, u32[]{:S(2)}) collective-permute-start(f32[1,32,1024]{2,1,0:T(8,128)S(1)} %get-tuple-element.22), channel_id=1, source_target_pairs={{1,0},{2,1},{3,2},{4,3},{5,4},{6,5},{7,6},{9,8},{10,9},{11,10},{12... | collective-permute-start | bytes 393224 | tf_op jit(solution)/shard_map/ppermute | solution.py:28
  6.8 4.2 %collective-permute-start.1 = (f32[1,32,1024]{2,1,0:T(8,128)S(1)}, f32[1,32,1024]{2,1,0:T(8,128)S(1)}, u32[]{:S(2)}, u32[]{:S(2)}) collective-permute-start(f32[1,32,1024]{2,1,0:T(8,128)S(1)} %get-tuple-element.21), channel_id=1, source_target_pairs={{0,1},{1,2},{2,3},{3,4},{4,5},{5,6},{6,7},{8,9},{9,10},{10,11},{11... | collective-permute-start | bytes 393224 | tf_op jit(solution)/shard_map/ppermute | solution.py:26
  11.0 0.7 copy-start.11
  11.7 2.6 %copy-start.1 = (bf16[3,1,16,32,1024]{4,3,2,1,0:T(8,128)(2,1)S(1)}, bf16[3,1,16,32,1024]{4,3,2,1,0:T(8,128)(2,1)}, u32[]{:S(2)}) copy-start(bf16[3,1,16,32,1024]{4,3,2,1,0:T(8,128)(2,1)} %param.9) | copy-start | bytes 9437188
  11.7 2.8 %copy-start.6 = (bf16[1,16,32,1024]{3,2,1,0:T(8,128)(2,1)S(1)}, bf16[1,16,32,1024]{3,2,1,0:T(8,128)(2,1)}, u32[]{:S(2)}) copy-start(bf16[1,16,32,1024]{3,2,1,0:T(8,128)(2,1)} %param.8) | copy-start | bytes 3145732
  11.7 2.8 %copy-start.12 = (f32[1,32,1024]{2,1,0:T(8,128)S(1)}, f32[1,32,1024]{2,1,0:T(8,128)}, u32[]{:S(2)}) copy-start(f32[1,32,1024]{2,1,0:T(8,128)} %copy-done.11) | copy-start | bytes 393220
  21.5 6.7 %collective-permute-start.2 = (f32[1,32,1024]{2,1,0:T(8,128)S(1)}, f32[1,32,1024]{2,1,0:T(8,128)S(1)}, u32[]{:S(2)}, u32[]{:S(2)}) collective-permute-start(f32[1,32,1024]{2,1,0:T(8,128)S(1)} %get-tuple-element.20), channel_id=1, source_target_pairs={{1,0},{2,1},{3,2},{4,3},{5,4},{6,5},{7,6},{9,8},{10,9},{11,10},{12... | collective-permute-start | bytes 393224 | tf_op jit(solution)/shard_map/ppermute | solution.py:28
  24.0 5.5 %collective-permute-start.3 = (f32[1,32,1024]{2,1,0:T(8,128)S(1)}, f32[1,32,1024]{2,1,0:T(8,128)S(1)}, u32[]{:S(2)}, u32[]{:S(2)}) collective-permute-start(f32[1,32,1024]{2,1,0:T(8,128)S(1)} %get-tuple-element.19), channel_id=1, source_target_pairs={{0,1},{1,2},{2,3},{3,4},{4,5},{5,6},{6,7},{8,9},{9,10},{10,11},{11... | collective-permute-start | bytes 393224 | tf_op jit(solution)/shard_map/ppermute | solution.py:26
  30.1 13.8 %copy-start.10 = (f32[1,256,128]{2,1,0:T(8,128)S(1)}, f32[1,256,128]{2,1,0:T(8,128)}, u32[]{:S(2)}) copy-start(f32[1,256,128]{2,1,0:T(8,128)} %param.12) | copy-start | bytes 393220
  35.5 1.3 copy-start.4
  37.6 7.3 %collective-permute-start.4 = (f32[1,32,1024]{2,1,0:T(8,128)}, f32[1,32,1024]{2,1,0:T(8,128)}, u32[]{:S(2)}, u32[]{:S(2)}) collective-permute-start(f32[1,32,1024]{2,1,0:T(8,128)} %get-tuple-element.18), channel_id=1, source_target_pairs={{1,0},{2,1},{3,2},{4,3},{5,4},{6,5},{7,6},{9,8},{10,9},{11,10},{12... | collective-permute-start | bytes 393224 | tf_op jit(solution)/shard_map/ppermute | solution.py:28
  39.5 6.6 %collective-permute-start.5 = (f32[1,32,1024]{2,1,0:T(8,128)}, f32[1,32,1024]{2,1,0:T(8,128)}, u32[]{:S(2)}, u32[]{:S(2)}) collective-permute-start(f32[1,32,1024]{2,1,0:T(8,128)} %get-tuple-element.17), channel_id=1, source_target_pairs={{0,1},{1,2},{2,3},{3,4},{4,5},{5,6},{6,7},{8,9},{9,10},{10,11},{11... | collective-permute-start | bytes 393224 | tf_op jit(solution)/shard_map/ppermute | solution.py:26
  44.6 3.7 %copy-start.5 = (f32[16,32,1024]{2,1,0:T(8,128)S(1)}, f32[16,32,1024]{2,1,0:T(8,128)}, u32[]{:S(2)}) copy-start(f32[16,32,1024]{2,1,0:T(8,128)} %copy-done.4) | copy-start | bytes 6291460
  44.6 3.7 %copy-start.7 = (bf16[1,16,32,1024]{3,2,1,0:T(8,128)(2,1)S(1)}, bf16[1,16,32,1024]{3,2,1,0:T(8,128)(2,1)}, u32[]{:S(2)}) copy-start(bf16[1,16,32,1024]{3,2,1,0:T(8,128)(2,1)} %param.8) | copy-start | bytes 3145732
  48.3 13.1 %copy-start.13 = (f32[1,256,128]{1,2,0:T(8,128)S(1)}, f32[1,256,128]{1,2,0:T(8,128)}, u32[]{:S(2)}) copy-start(f32[1,256,128]{1,2,0:T(8,128)} %copy.21) | copy-start | bytes 393220
  53.0 1.3 copy-start.2
  55.1 10.9 %collective-permute-start.6 = (f32[1,32,1024]{2,1,0:T(8,128)}, f32[1,32,1024]{2,1,0:T(8,128)}, u32[]{:S(2)}, u32[]{:S(2)}) collective-permute-start(f32[1,32,1024]{2,1,0:T(8,128)} %get-tuple-element.16), channel_id=1, source_target_pairs={{1,0},{2,1},{3,2},{4,3},{5,4},{6,5},{7,6},{9,8},{10,9},{11,10},{12... | collective-permute-start | bytes 393224 | tf_op jit(solution)/shard_map/ppermute | solution.py:28
  57.0 9.0 %collective-permute-start.7 = (f32[1,32,1024]{2,1,0:T(8,128)}, f32[1,32,1024]{2,1,0:T(8,128)}, u32[]{:S(2)}, u32[]{:S(2)}) collective-permute-start(f32[1,32,1024]{2,1,0:T(8,128)} %get-tuple-element.15), channel_id=1, source_target_pairs={{0,1},{1,2},{2,3},{3,4},{4,5},{5,6},{6,7},{8,9},{9,10},{10,11},{11... | collective-permute-start | bytes 393224 | tf_op jit(solution)/shard_map/ppermute | solution.py:26
  62.3 19.8 %all-to-all-start.1 = ((f32[8,16,128]{2,1,0:T(8,128)}), f32[8,16,128]{2,1,0:T(8,128)S(1)}, u32[]{:S(2)}, u32[]{:S(2)}) async-start(f32[8,16,128]{2,1,0:T(8,128)} %fusion.37), calls=%async_computation.1 | async-start | bytes 131072 | tf_op jit(solution)/shard_map/all_to_all | solution.py:50
  66.0 2.4 %copy-start.3 = (f32[16,32,1024]{2,1,0:T(8,128)S(1)}, f32[16,32,1024]{2,1,0:T(8,128)}, u32[]{:S(2)}) copy-start(f32[16,32,1024]{2,1,0:T(8,128)} %copy-done.2) | copy-start | bytes 6291460
  66.0 2.6 %copy-start.8 = (bf16[1,16,32,1024]{3,2,1,0:T(8,128)(2,1)S(1)}, bf16[1,16,32,1024]{3,2,1,0:T(8,128)(2,1)}, u32[]{:S(2)}) copy-start(bf16[1,16,32,1024]{3,2,1,0:T(8,128)(2,1)} %param.8) | copy-start | bytes 3145732
  68.6 36.0 %copy-start.14 = (s32[1,256]{1,0:T(1,128)S(1)}, s32[1,256]{1,0:T(1,128)}, u32[]{:S(2)}) copy-start(s32[1,256]{1,0:T(1,128)} %param.11) | copy-start | bytes 3076
  73.3 1.3 copy-start.9
  74.6 47.5 %copy-start.15 = (f32[1,256]{1,0:T(1,128)S(1)}, f32[1,256]{1,0:T(1,128)}, u32[]{:S(2)}) copy-start(f32[1,256]{1,0:T(1,128)} %param.10) | copy-start | bytes 3076
  75.1 7.9 %collective-permute-start.8 = (f32[1,256]{1,0:T(1,128)S(1)}, f32[1,256]{1,0:T(1,128)S(1)}, u32[]{:S(2)}, u32[]{:S(2)}) collective-permute-start(f32[1,256]{1,0:T(1,128)S(1)} %div.18), channel_id=1, source_target_pairs={{0,128},{8,136},{16,144},{24,152},{32,160},{40,168},{48,176},{56,1... | collective-permute-start | bytes 3080 | tf_op jit(solution)/shard_map/ppermute | solution.py:38
  83.6 10.3 %all-to-all-start = ((f32[8,1,256]{2,1,0:T(1,128)}), f32[8,1,256]{2,1,0:T(1,128)S(1)}, u32[]{:S(2)}, u32[]{:S(2)}) async-start(f32[8,1,256]{2,1,0:T(1,128)} %stack.2), calls=%async_computation | async-start | bytes 16384 | tf_op jit(solution)/shard_map/all_to_all | solution.py:14
  94.6 21.2 %all-to-all-start.2 = ((f32[32,16,128]{2,1,0:T(8,128)}), f32[32,16,128]{2,1,0:T(8,128)S(1)}, u32[]{:S(2)}, u32[]{:S(2)}) async-start(f32[32,16,128]{2,1,0:T(8,128)} %broadcast_in_dim.51), calls=%async_computation.2 | async-start | bytes 524288 | tf_op jit(solution)/shard_map/all_to_all | solution.py:44
  116.4 10.6 %all-to-all-start.3 = ((f32[8,16,128]{2,1,0:T(8,128)}), f32[8,16,128]{2,1,0:T(8,128)S(1)}, u32[]{:S(2)}, u32[]{:S(2)}) async-start(f32[8,16,128]{2,1,0:T(8,128)} %broadcast_in_dim.52), calls=%async_computation.3 | async-start | bytes 131072 | tf_op jit(solution)/shard_map/all_to_all | solution.py:53
  127.7 29.9 %all-to-all-start.4 = ((f32[256,1,128]{2,1,0:T(1,128)}), f32[256,1,128]{2,1,0:T(1,128)S(1)}, u32[]{:S(2)}, u32[]{:S(2)}) async-start(f32[256,1,128]{2,1,0:T(1,128)} %broadcast_in_dim.54), calls=%async_computation.4 | async-start | bytes 262144 | tf_op jit(solution)/shard_map/all_to_all | solution.py:44
